TPU v7x, 32 devices: a whole 2x2x4 slice. The times are simulated.
32 devices in a mesh: rep: 2 (over x), exp: 4 (over y, core), shard: 4 (over z).
Axes of the slice: x: 2, y: 2, z: 4, core: 2. Of those that a mesh axis runs over, the one named last changes fastest.
Arguments:
- deltas: bfloat16 [2, 4, 2048, 7168], P('rep', 'exp', 'shard'), may hold values from -0.1875 to 0.1875
- master: float32 [4, 2048, 7168], P('exp', 'shard', 'rep'), may hold values from -0.125 to 0.125
- momentum: float32 [4, 2048, 7168], P('exp', 'shard', 'rep'), may hold values from -0.12 to 0.12
- tokens: bfloat16 [4, 2048, 2048], P('exp', 'shard'), may hold values from -6 to 6
Outputs:
- new_master: float32 [4, 2048, 7168], P('exp', 'shard', 'rep')
- new_momentum: float32 [4, 2048, 7168], P('exp', 'shard', 'rep')
- probe_out: bfloat16 [4, 2048, 7168], P('exp', 'shard', 'rep')
All inputs are finite; a program needn't handle non-finite values.
Results may differ from a plain program's by a relative error of at most 0.014.
Values may be sent and summed in bfloat16 or wider, within the bound.
A program may use at most 128 MiB of HBM per device.

v0:
```python
import jax
import jax.numpy as jnp
from jax import lax
from jax.sharding import PartitionSpec as P

outer_rate = 0.7
momentum_coef = 0.9


def body(deltas, master, momentum, tokens):
    summed = lax.psum_scatter(
        deltas[0, 0].astype(jnp.float32).astype(jnp.bfloat16),
        "rep",
        scatter_dimension=1,
        tiled=True,
    ).astype(jnp.float32)
    outer_grad = summed / lax.axis_size("rep")
    new_momentum = momentum_coef * momentum[0] + outer_grad
    new_master = master[0] - outer_rate * (outer_grad + momentum_coef * new_momentum)
    weight_bf = new_master.astype(jnp.bfloat16)
    local_tokens = tokens[0]
    token_cols = lax.all_to_all(local_tokens, "shard", split_axis=1, concat_axis=0, tiled=True)
    projected = lax.psum_scatter(
        jnp.dot(token_cols, weight_bf, preferred_element_type=jnp.float32).astype(jnp.bfloat16),
        "shard",
        scatter_dimension=0,
        tiled=True,
    )
    return (new_master[None], new_momentum[None], projected[None])


def solution(mesh):
    placed = (
        P("rep", "exp", "shard", None),
        P("exp", "shard", "rep"),
        P("exp", "shard", "rep"),
        P("exp", "shard", None),
    )
    return jax.shard_map(
        body,
        mesh=mesh,
        in_specs=placed,
        out_specs=(P("exp", "shard", "rep"), P("exp", "shard", "rep"), P("exp", "shard", "rep")),
        check_vma=False,
    )
```

profile of v0, /device:TPU:0, one launch (start us, length us, event | category | flops | bytes accessed | tf_op | source)
XLA Modules:
  0.0 380.0 jit_solution(6621440800665003920)
XLA Ops:
  7.2 0.0 copy-start
  7.2 0.0 reduce-scatter.3.cloned.1.call-start
  7.2 0.7 reduce-scatter.3.cloned.1.call-update
  7.9 0.0 reduce-scatter.5.cloned.1.call-start
  8.0 0.8 copy-done
  8.8 2.5 copy.9
  11.2 54.5 %all_to_all.19 = bf16[512,4,512]{0,2,1:T(8,128)(2,1)S(1)} all-to-all(bf16[512,4,512]{0,2,1:T(8,128)(2,1)} %bitcast.31), channel_id=1, replica_groups=mesh['rep'=2,'exp'=4,'shard'=4] {'shard'}, dimensions={1} | all-to-all | bytes 4194304 | tf_op jit(solution)/shard_map/all_to_all | solution.py:22
  65.8 2.4 copy.10
  68.1 33.4 %reduce-scatter.3.cloned.1.call-done = bf16[512,3584]{1,0:T(8,128)(2,1)} async-done(((bf16[512,7168]{1,0:T(8,128)(2,1)}), bf16[512,3584]{1,0:T(8,128)(2,1)}) %reduce-scatter.3.cloned.1.call-update) | async-done | bytes 3670032 | tf_op jit(solution)/shard_map/reduce_scatter | solution.py:11
  101.5 19.8 %fusion = bf16[2048,3584]{0,1:T(8,128)(2,1)} fusion(bf16[2048,512]{1,0:T(8,128)(2,1)} %bitcast.34, f32[1,512,3584]{2,1,0:T(8,128)} %param.5, bf16[512,3584]{1,0:T(8,128)(2,1)} %reduce-scatter.3.cloned.1.call-done, f32[1,512,3584]{2,1,0:T(8,128)} %param.6), kind=kOutput, calls=%fused_computation.1 | convolution fusion | flops 7540047872 | bytes 35127296 | tf_op jit(solution)/shard_map/dot_general | solution.py:24
  121.3 0.0 reduce-scatter.5.cloned.1.call-update
  121.3 11.6 %fusion.1 = (f32[1,512,3584]{2,1,0:T(8,128)}, f32[1,512,3584]{2,1,0:T(8,128)}) fusion(bf16[512,3584]{1,0:T(8,128)(2,1)} %reduce-scatter.3.cloned.1.call-done, f32[1,512,3584]{2,1,0:T(8,128)} %param.6, f32[1,512,3584]{2,1,0:T(8,128)} %param.5), kind=kLoop, calls=%fused_computation.5 | loop fusion | flops 14680064 | bytes 33030144 | tf_op jit(solution)/shard_map/broadcast_in_dim | solution.py:29
  133.0 234.2 %reduce-scatter.5.cloned.1.call-done = bf16[512,3584]{0,1:T(8,128)(2,1)} async-done(((bf16[2048,3584]{0,1:T(8,128)(2,1)}), bf16[512,3584]{0,1:T(8,128)(2,1)}) %reduce-scatter.5.cloned.1.call-update) | async-done | bytes 3670032 | tf_op jit(solution)/shard_map/reduce_scatter | solution.py:23
  367.2 5.9 %copy.11 = bf16[1,512,3584]{2,1,0:T(8,128)(2,1)} copy(bf16[1,512,3584]{1,2,0:T(8,128)(2,1)} %bitcast.33) | data formatting | bytes 7340032
Async XLA Ops:
  7.2 1.6 copy-start
  7.2 94.4 %reduce-scatter.3.cloned.1.call-start = ((), (), s32[]{:S(2)}) async-start(), calls=%async_computation.3 | async-start | bytes 11010048 | tf_op jit(solution)/shard_map/reduce_scatter | solution.py:11
  7.9 359.3 %reduce-scatter.5.cloned.1.call-start = ((), (), s32[]{:S(2)}) async-start(), calls=%async_computation.4 | async-start | bytes 18350080 | tf_op jit(solution)/shard_map/reduce_scatter | solution.py:23
Sparse Core Ops, SparseCore 0:
  10.3 91.2 reduce-scatter.2
  121.5 245.7 reduce-scatter.4
where the time goes:
time: 380 us
  waiting for transfers between devices  268 us (71%)
  blocking collectives  54.5 us (14%)
  matrix products  19.8 us (5%)
  between operations  14 us (4%)
  local copies, waits for them, and re-layouts  11.6 us (3%)
  other arithmetic  11.6 us (3%)
    reduce_scatter x1, waiting for transfers between devices, body(): lax.psum_scatter(jnp.dot(token_cols, weight_bf, preferred_element_type=jn...  234 us
    all_to_all x1, blocking collectives, body(): lax.all_to_all(local_tokens, 'shard', split_axis=1, concat_axis=0, tiled=...  54.5 us
    reduce_scatter x1, waiting for transfers between devices, body(): lax.psum_scatter(deltas[0, 0].astype(jnp.float32).astype(jnp.bfloat16), '...  33.4 us
    dot_general x1, matrix products, body(): jnp.dot(token_cols, weight_bf, preferred_element_type=jnp.float32)  19.8 us
    broadcast_in_dim x1, other arithmetic, body(): return (new_master[None], new_momentum[None], projected[None])  11.6 us
    unnamed x4, local copies, waits for them, and re-layouts  9.2 us
  transfers between devices with their start and end apart: 2, of which 2 were waited for; matrix products, arithmetic and copies ran while one was open for 4% of the time, Pallas kernels for 0%

commit v1 on v0

--- a/solution.py
+++ b/solution.py
@@ -1,13 +1,22 @@
+import functools
+
 import jax
 import jax.numpy as jnp
 from jax import lax
+from jax.experimental import pallas as pl
+from jax.experimental.pallas import tpu as pltpu
 from jax.sharding import PartitionSpec as P
 
 outer_rate = 0.7
 momentum_coef = 0.9
-
-
-def body(deltas, master, momentum, tokens):
+MESH = pl.DeviceIdType.MESH
+CHUNK = 128
+AHEAD = 6
+TRAIL = 3
+ROWS = 256
+
+
+def plain_body(deltas, master, momentum, tokens):
     summed = lax.psum_scatter(
         deltas[0, 0].astype(jnp.float32).astype(jnp.bfloat16),
         "rep",
@@ -29,6 +38,237 @@
     return (new_master[None], new_momentum[None], projected[None])
 
 
+def line_kernel(
+    chunk, lag,
+    delta_hbm, master_hbm, momentum_hbm, token_hbm,
+    new_master_hbm, new_momentum_hbm, probe_hbm,
+    theirs, mine, master, momentum, weight, token, probe,
+    pair_send, pair_recv, load_sem, store_sem,
+    weight_send, weight_recv, pass_send, token_send, token_recv, token_load,
+    probe_send, probe_recv, probe_store,
+):
+    count, rows, _ = theirs.shape
+    half = count * chunk
+    r = lax.axis_index("rep")
+    z = lax.axis_index("shard")
+    twin = {"rep": 1 - r}
+    mate_at = z + 1 - 2 * lax.rem(z, 2)
+    across_at = 3 - z
+    mate = {"shard": mate_at}
+    across = {"shard": across_at}
+    inner = jnp.logical_and(z > 0, z < 3)
+    outer = jnp.logical_not(inner)
+
+    def columns(i):
+        return pl.ds(pl.multiple_of(i * chunk, chunk), chunk)
+
+    def half_columns(which, i):
+        return pl.ds(pl.multiple_of(which * half + i * chunk, chunk), chunk)
+
+    def loads(i):
+        return (
+            pltpu.make_async_copy(delta_hbm.at[:, half_columns(r, i)], mine.at[i], load_sem.at[0, i]),
+            pltpu.make_async_copy(master_hbm.at[:, columns(i)], master.at[i], load_sem.at[1, i]),
+            pltpu.make_async_copy(momentum_hbm.at[:, columns(i)], momentum.at[i], load_sem.at[2, i]),
+        )
+
+    def pair_copy(i):
+        return pltpu.make_async_remote_copy(
+            src_ref=delta_hbm.at[:, half_columns(1 - r, i)],
+            dst_ref=theirs.at[i],
+            send_sem=pair_send,
+            recv_sem=pair_recv.at[i],
+            device_id=twin,
+            device_id_type=MESH,
+        )
+
+    def weight_copy(block, i, send_sem, slot, target):
+        return pltpu.make_async_remote_copy(
+            src_ref=weight.at[block, i],
+            dst_ref=weight.at[block, i],
+            send_sem=send_sem,
+            recv_sem=weight_recv.at[slot, i],
+            device_id=target,
+            device_id_type=MESH,
+        )
+
+    def token_copy():
+        return pltpu.make_async_remote_copy(
+            src_ref=token_hbm,
+            dst_ref=token.at[1],
+            send_sem=token_send,
+            recv_sem=token_recv,
+            device_id=mate,
+            device_id_type=MESH,
+        )
+
+    def probe_copy(j):
+        return pltpu.make_async_remote_copy(
+            src_ref=probe.at[1, j],
+            dst_ref=probe_hbm.at[:, columns(j)],
+            send_sem=probe_send,
+            recv_sem=probe_recv,
+            device_id=mate,
+            device_id_type=MESH,
+        )
+
+    barrier = pltpu.get_barrier_semaphore()
+    pl.semaphore_signal(barrier, inc=1, device_id=twin, device_id_type=MESH)
+    pl.semaphore_signal(barrier, inc=1, device_id=mate, device_id_type=MESH)
+
+    @pl.when(inner)
+    def _():
+        pl.semaphore_signal(barrier, inc=1, device_id=across, device_id_type=MESH)
+        pl.semaphore_wait(barrier, 3)
+
+    @pl.when(outer)
+    def _():
+        pl.semaphore_wait(barrier, 2)
+
+    @pl.loop(0, AHEAD)
+    def _(i):
+        pair_copy(i).start()
+        for copy in loads(i):
+            copy.start()
+
+    @pl.when(outer)
+    def _():
+        token_copy().start()
+
+    own_tokens = pltpu.make_async_copy(token_hbm, token.at[0], token_load)
+
+    @pl.when(inner)
+    def _():
+        own_tokens.start()
+
+    @pl.loop(0, count + lag + TRAIL)
+    def _(i):
+        @pl.when(i + AHEAD < count)
+        def _():
+            pair_copy(i + AHEAD).start()
+            for copy in loads(i + AHEAD):
+                copy.start()
+
+        @pl.when(i < count)
+        def _():
+            for copy in loads(i):
+                copy.wait()
+            pair_copy(i).wait_recv()
+            outer_grad = (mine[i].astype(jnp.float32) + theirs[i].astype(jnp.float32)) * 0.5
+            new_momentum = momentum_coef * momentum[i] + outer_grad
+            new_master = master[i] - outer_rate * (outer_grad + momentum_coef * new_momentum)
+            weight[z, i] = new_master.astype(jnp.bfloat16)
+            master[i] = new_master
+            momentum[i] = new_momentum
+
+            @pl.when(inner)
+            def _():
+                weight_copy(z, i, weight_send, 1, across).start()
+
+            @pl.when(outer)
+            def _():
+                weight_copy(z, i, weight_send, 0, mate).start()
+
+            pltpu.make_async_copy(master.at[i], new_master_hbm.at[:, columns(i)], store_sem.at[0]).start()
+            pltpu.make_async_copy(momentum.at[i], new_momentum_hbm.at[:, columns(i)], store_sem.at[1]).start()
+
+        j = i - lag
+
+        @pl.when(jnp.logical_and(inner, jnp.logical_and(j >= 0, j < count)))
+        def _():
+            weight_copy(mate_at, j, pass_send, 0, across).wait_recv()
+            weight_copy(mate_at, j, pass_send, 2, across).start()
+
+        k = i - lag - TRAIL
+
+        @pl.when(jnp.logical_and(inner, k >= 0))
+        def _():
+            @pl.when(k == 0)
+            def _():
+                own_tokens.wait()
+                token_copy().wait_recv()
+
+            weight_copy(across_at, k, weight_send, 1, across).wait_recv()
+            weight_copy(3 - mate_at, k, pass_send, 2, across).wait_recv()
+            for owner in range(2):
+                @pl.loop(0, rows // ROWS)
+                def _(b):
+                    span = pl.ds(pl.multiple_of(b * ROWS, ROWS), ROWS)
+                    total = jnp.zeros((ROWS, chunk), jnp.float32)
+                    for block in range(4):
+                        total += jnp.dot(
+                            token[owner, span, block * rows:(block + 1) * rows],
+                            weight[block, k],
+                            preferred_element_type=jnp.float32,
+                        )
+                    probe[owner, k, span, :] = total.astype(jnp.bfloat16)
+
+            probe_copy(k).start()
+            pltpu.make_async_copy(probe.at[0, k], probe_hbm.at[:, columns(k)], probe_store).start()
+
+    pltpu.make_async_copy(theirs, theirs, pair_send).wait()
+    pltpu.make_async_copy(weight.at[0], weight.at[0], weight_send).wait()
+    pltpu.make_async_copy(master, master, store_sem.at[0]).wait()
+    pltpu.make_async_copy(momentum, momentum, store_sem.at[1]).wait()
+
+    @pl.when(inner)
+    def _():
+        pltpu.make_async_copy(weight.at[0], weight.at[0], pass_send).wait()
+        pltpu.make_async_copy(probe.at[0], probe.at[0], probe_send).wait()
+        pltpu.make_async_copy(probe.at[0], probe.at[0], probe_store).wait()
+
+    @pl.when(outer)
+    def _():
+        token_copy().wait_send()
+        pltpu.make_async_copy(probe_hbm, probe_hbm, probe_recv).wait()
+
+
+def line_body(deltas, master, momentum, tokens):
+    rows, half = master.shape[1:]
+    width = tokens.shape[2]
+    count = half // CHUNK
+    lag = width // CHUNK
+    bf16, f32 = jnp.bfloat16, jnp.float32
+    dma = pltpu.SemaphoreType.DMA
+    anywhere = pl.BlockSpec(memory_space=pl.ANY)
+    new_master, new_momentum, probe = pl.pallas_call(
+        functools.partial(line_kernel, CHUNK, lag),
+        out_shape=(
+            jax.ShapeDtypeStruct((rows, half), f32),
+            jax.ShapeDtypeStruct((rows, half), f32),
+            jax.ShapeDtypeStruct((rows, half), bf16),
+        ),
+        in_specs=[anywhere] * 4,
+        out_specs=(anywhere,) * 3,
+        scratch_shapes=[
+            pltpu.VMEM((count, rows, CHUNK), bf16),
+            pltpu.VMEM((count, rows, CHUNK), bf16),
+            pltpu.VMEM((count, rows, CHUNK), f32),
+            pltpu.VMEM((count, rows, CHUNK), f32),
+            pltpu.VMEM((4, count, rows, CHUNK), bf16),
+            pltpu.VMEM((2, rows, width), bf16),
+            pltpu.VMEM((2, count, rows, CHUNK), bf16),
+            dma,
+            dma((count,)),
+            dma((3, count)),
+            dma((2,)),
+            dma,
+            dma((3, count)),
+            dma,
+            dma,
+            dma,
+            dma,
+            dma,
+            dma,
+            dma,
+        ],
+        compiler_params=pltpu.CompilerParams(
+            collective_id=0, has_side_effects=True, vmem_limit_bytes=60 * 1024 * 1024
+        ),
+    )(deltas[0, 0], master[0], momentum[0], tokens[0])
+    return (new_master[None], new_momentum[None], probe[None])
+
+
 def solution(mesh):
     placed = (
         P("rep", "exp", "shard", None),
@@ -36,8 +276,9 @@
         P("exp", "shard", "rep"),
         P("exp", "shard", None),
     )
+    paired = mesh.shape["rep"] == 2 and mesh.shape["shard"] == 4
     return jax.shard_map(
-        body,
+        line_body if paired else plain_body,
         mesh=mesh,
         in_specs=placed,
         out_specs=(P("exp", "shard", "rep"), P("exp", "shard", "rep"), P("exp", "shard", "rep")),

time: 380 us -> 191 us (0.50)
  waiting for transfers between devices: 268 us -> 0 us
  Pallas kernels: 0 us -> 177 us
  blocking collectives: 54.5 us -> 0 us
  matrix products: 19.8 us -> 0 us
  between operations: 14 us -> 0.65 us
  other arithmetic: 11.6 us -> 0 us
    reduce_scatter x2 -> x0, waiting for transfers between devices: 268 us -> none  [the longest x1 234 us: body(): lax.psum_scatter(jnp.dot(token_cols, weight_bf, preferred_element_type=jn...]
    pallas_call x0 -> x1, Pallas kernels: none -> 177 us  [line_body(): pl.pallas_call(functools.partial(line_kernel, CHUNK, lag), out_shape=(jax...]
    all_to_all x1 -> x0, blocking collectives: 54.5 us -> none  [body(): lax.all_to_all(local_tokens, 'shard', split_axis=1, concat_axis=0, tiled=...]
    dot_general x1 -> x0, matrix products: 19.8 us -> none  [body(): jnp.dot(token_cols, weight_bf, preferred_element_type=jnp.float32)]
    broadcast_in_dim x1 -> x0, other arithmetic: 11.6 us -> none  [body(): return (new_master[None], new_momentum[None], projected[None])]
    unnamed x4 -> x7, local copies, waits for them, and re-layouts: 9.2 us -> 13.3 us
  transfers between devices with their start and end apart: 2 -> 0, of which waited for: 2 -> 0; matrix products, arithmetic and copies ran while one was open for 4% -> 0% of each run, Pallas kernels for 0% -> 0%
where the time goes in v1:
time: 191 us
  Pallas kernels  177 us (93%)
  local copies, waits for them, and re-layouts  13.3 us (7%)
    pallas_call x1, Pallas kernels, line_body(): pl.pallas_call(functools.partial(line_kernel, CHUNK, lag), out_shape=(jax...  177 us
    unnamed x7, local copies, waits for them, and re-layouts  13.3 us

profile of v1, /device:TPU:0, one launch (start us, length us, event | category | flops | bytes accessed | tf_op | source)
XLA Modules:
  0.0 191.1 jit_solution(14697327601114655137)
XLA Ops:
  0.6 177.2 %shard_map.67 = (f32[512,3584]{1,0:T(8,128)}, f32[512,3584]{1,0:T(8,128)}, bf16[512,3584]{1,0:T(8,128)(2,1)}) custom-call(bf16[512,7168]{1,0:T(8,128)(2,1)} %bitcast.9, f32[512,3584]{1,0:T(8,128)} %bitcast.10, f32[512,3584]{1,0:T(8,128)} %bitcast.11, bf16[512,2048]{1,0:T(8,128)(2,1)} %bitcast.13), custom_call_target="tpu_custom_call" | custom-call | tf_op jit(solution)/shard_map/pallas_call | solution.py:234
  177.8 0.0 copy-start
  177.8 6.8 %copy.10 = f32[1,512,3584]{2,1,0:T(8,128)} copy(f32[1,512,3584]{2,1,0:T(8,128)} %bitcast.8) | data formatting | bytes 14680064
  184.6 0.0 copy-done
  184.6 0.0 copy-start.1
  184.6 3.7 %copy.11 = f32[1,512,3584]{2,1,0:T(8,128)} copy(f32[1,512,3584]{2,1,0:T(8,128)S(1)} %bitcast.7) | data formatting | bytes 14680064
  188.3 1.0 copy-done.1
  189.3 1.8 copy.12
Async XLA Ops:
  177.8 6.8 %copy-start = (f32[512,3584]{1,0:T(8,128)S(1)}, f32[512,3584]{1,0:T(8,128)}, u32[]{:S(2)}) copy-start(f32[512,3584]{1,0:T(8,128)} %get-tuple-element.7) | copy-start | bytes 22020100
  184.6 4.7 %copy-start.1 = (bf16[512,3584]{1,0:T(8,128)(2,1)S(1)}, bf16[512,3584]{1,0:T(8,128)(2,1)}, u32[]{:S(2)}) copy-start(bf16[512,3584]{1,0:T(8,128)(2,1)} %get-tuple-element.8) | copy-start | bytes 11010052

commit v2 on v1

--- a/solution.py
+++ b/solution.py
@@ -41,11 +41,11 @@
 def line_kernel(
     chunk, lag,
     delta_hbm, master_hbm, momentum_hbm, token_hbm,
-    new_master_hbm, new_momentum_hbm, probe_hbm,
-    theirs, mine, master, momentum, weight, token, probe,
-    pair_send, pair_recv, load_sem, store_sem,
+    master, momentum, probe,
+    theirs, mine, weight, token, mate_probe,
+    pair_send, pair_recv, load_sem,
     weight_send, weight_recv, pass_send, token_send, token_recv, token_load,
-    probe_send, probe_recv, probe_store,
+    probe_send, probe_recv,
 ):
     count, rows, _ = theirs.shape
     half = count * chunk
@@ -104,8 +104,8 @@
 
     def probe_copy(j):
         return pltpu.make_async_remote_copy(
-            src_ref=probe.at[1, j],
-            dst_ref=probe_hbm.at[:, columns(j)],
+            src_ref=mate_probe.at[j],
+            dst_ref=probe.at[j],
             send_sem=probe_send,
             recv_sem=probe_recv,
             device_id=mate,
@@ -169,9 +169,6 @@
             def _():
                 weight_copy(z, i, weight_send, 0, mate).start()
 
-            pltpu.make_async_copy(master.at[i], new_master_hbm.at[:, columns(i)], store_sem.at[0]).start()
-            pltpu.make_async_copy(momentum.at[i], new_momentum_hbm.at[:, columns(i)], store_sem.at[1]).start()
-
         j = i - lag
 
         @pl.when(jnp.logical_and(inner, jnp.logical_and(j >= 0, j < count)))
@@ -190,7 +187,7 @@
 
             weight_copy(across_at, k, weight_send, 1, across).wait_recv()
             weight_copy(3 - mate_at, k, pass_send, 2, across).wait_recv()
-            for owner in range(2):
+            for owner, result in enumerate((probe, mate_probe)):
                 @pl.loop(0, rows // ROWS)
                 def _(b):
                     span = pl.ds(pl.multiple_of(b * ROWS, ROWS), ROWS)
@@ -201,26 +198,34 @@
                             weight[block, k],
                             preferred_element_type=jnp.float32,
                         )
-                    probe[owner, k, span, :] = total.astype(jnp.bfloat16)
+                    result[k, span, :] = total.astype(jnp.bfloat16)
 
             probe_copy(k).start()
-            pltpu.make_async_copy(probe.at[0, k], probe_hbm.at[:, columns(k)], probe_store).start()
 
     pltpu.make_async_copy(theirs, theirs, pair_send).wait()
     pltpu.make_async_copy(weight.at[0], weight.at[0], weight_send).wait()
-    pltpu.make_async_copy(master, master, store_sem.at[0]).wait()
-    pltpu.make_async_copy(momentum, momentum, store_sem.at[1]).wait()
 
     @pl.when(inner)
     def _():
         pltpu.make_async_copy(weight.at[0], weight.at[0], pass_send).wait()
-        pltpu.make_async_copy(probe.at[0], probe.at[0], probe_send).wait()
-        pltpu.make_async_copy(probe.at[0], probe.at[0], probe_store).wait()
+        pltpu.make_async_copy(mate_probe, mate_probe, probe_send).wait()
 
     @pl.when(outer)
     def _():
         token_copy().wait_send()
-        pltpu.make_async_copy(probe_hbm, probe_hbm, probe_recv).wait()
+        pltpu.make_async_copy(probe, probe, probe_recv).wait()
+
+
+def store_kernel(chunk, *refs):
+    copies = []
+    for at in range(3):
+        source, target, sem = refs[at], refs[3 + at], refs[6].at[at]
+        for i in range(source.shape[0]):
+            copies.append(pltpu.make_async_copy(source.at[i], target.at[:, pl.ds(i * chunk, chunk)], sem))
+    for copy in copies:
+        copy.start()
+    for at in range(3):
+        pltpu.make_async_copy(refs[at], refs[at], refs[6].at[at]).wait()
 
 
 def line_body(deltas, master, momentum, tokens):
@@ -231,41 +236,47 @@
     bf16, f32 = jnp.bfloat16, jnp.float32
     dma = pltpu.SemaphoreType.DMA
     anywhere = pl.BlockSpec(memory_space=pl.ANY)
+    local = pl.BlockSpec(memory_space=pltpu.VMEM)
+    blocks = (count, rows, CHUNK)
+    results = pl.pallas_call(
+        functools.partial(line_kernel, CHUNK, lag),
+        out_shape=(pltpu.VMEM(blocks, f32), pltpu.VMEM(blocks, f32), pltpu.VMEM(blocks, bf16)),
+        in_specs=[anywhere] * 4,
+        out_specs=(local,) * 3,
+        scratch_shapes=[
+            pltpu.VMEM(blocks, bf16),
+            pltpu.VMEM(blocks, bf16),
+            pltpu.VMEM((4,) + blocks, bf16),
+            pltpu.VMEM((2, rows, width), bf16),
+            pltpu.VMEM(blocks, bf16),
+            dma,
+            dma((count,)),
+            dma((3, count)),
+            dma,
+            dma((3, count)),
+            dma,
+            dma,
+            dma,
+            dma,
+            dma,
+            dma,
+        ],
+        compiler_params=pltpu.CompilerParams(
+            collective_id=0, has_side_effects=True, vmem_limit_bytes=45 * 1024 * 1024
+        ),
+    )(deltas[0, 0], master[0], momentum[0], tokens[0])
     new_master, new_momentum, probe = pl.pallas_call(
-        functools.partial(line_kernel, CHUNK, lag),
+        functools.partial(store_kernel, CHUNK),
         out_shape=(
             jax.ShapeDtypeStruct((rows, half), f32),
             jax.ShapeDtypeStruct((rows, half), f32),
             jax.ShapeDtypeStruct((rows, half), bf16),
         ),
-        in_specs=[anywhere] * 4,
+        in_specs=[local] * 3,
         out_specs=(anywhere,) * 3,
-        scratch_shapes=[
-            pltpu.VMEM((count, rows, CHUNK), bf16),
-            pltpu.VMEM((count, rows, CHUNK), bf16),
-            pltpu.VMEM((count, rows, CHUNK), f32),
-            pltpu.VMEM((count, rows, CHUNK), f32),
-            pltpu.VMEM((4, count, rows, CHUNK), bf16),
-            pltpu.VMEM((2, rows, width), bf16),
-            pltpu.VMEM((2, count, rows, CHUNK), bf16),
-            dma,
-            dma((count,)),
-            dma((3, count)),
-            dma((2,)),
-            dma,
-            dma((3, count)),
-            dma,
-            dma,
-            dma,
-            dma,
-            dma,
-            dma,
-            dma,
-        ],
-        compiler_params=pltpu.CompilerParams(
-            collective_id=0, has_side_effects=True, vmem_limit_bytes=60 * 1024 * 1024
-        ),
-    )(deltas[0, 0], master[0], momentum[0], tokens[0])
+        scratch_shapes=[dma((3,))],
+        compiler_params=pltpu.CompilerParams(vmem_limit_bytes=1024 * 1024),
+    )(*results)
     return (new_master[None], new_momentum[None], probe[None])
 
 

time: 191 us -> 184 us (0.963)
  local copies, waits for them, and re-layouts: 13.3 us -> 0 us
  Pallas kernels: 177 us -> 183 us
    unnamed x7 -> x0, local copies, waits for them, and re-layouts: 13.3 us -> none
    pallas_call x1 -> x2, Pallas kernels: 177 us -> 183 us  [the longest x1 177 us: line_body(): pl.pallas_call(functools.partial(line_kernel, CHUNK, lag), out_shape=(plt...]
where the time goes in v2:
time: 184 us
  Pallas kernels  183 us (99%)
    pallas_call x1, Pallas kernels, line_body(): pl.pallas_call(functools.partial(line_kernel, CHUNK, lag), out_shape=(plt...  177 us
    pallas_call x1, Pallas kernels, line_body(): pl.pallas_call(functools.partial(store_kernel, CHUNK), out_shape=(jax.Sha...  6.25 us

profile of v2, /device:TPU:0, one launch (start us, length us, event | category | flops | bytes accessed | tf_op | source)
XLA Modules:
  0.0 183.9 jit_solution(16047895737889811810)
XLA Ops:
  0.6 177.1 %shard_map.67 = (f32[28,512,128]{2,1,0:T(8,128)S(1)}, f32[28,512,128]{2,1,0:T(8,128)S(1)}, bf16[28,512,128]{2,1,0:T(8,128)(2,1)S(1)}) custom-call(bf16[512,7168]{1,0:T(8,128)(2,1)} %bitcast.7, f32[512,3584]{1,0:T(8,128)} %bitcast.8, f32[512,3584]{1,0:T(8,128)} %bitcast.9, bf16[512,2048]{1,0:T(8,128)(2,1)} %bitcast.10), custom_call_target="tpu_custom_call" | custom-call | tf_op jit(solution)/shard_map/pallas_call | solution.py:241
  177.7 6.2 %shard_map.68 = (f32[512,3584]{1,0:T(8,128)}, f32[512,3584]{1,0:T(8,128)}, bf16[512,3584]{1,0:T(8,128)(2,1)}) custom-call(f32[28,512,128]{2,1,0:T(8,128)S(1)} %get-tuple-element.9.refs_0_, f32[28,512,128]{2,1,0:T(8,128)S(1)} %get-tuple-element.10.refs_1_, bf16[28,512,128]{2,1,0:T(8,128)(2,1)S(1)} %get-tuple-element.11.refs_2_), custom_call_target="tpu_custom_call" | custom-call | tf_op jit(solution)/shard_map/pallas_call | solution.py:268

commit v3 on v2

--- a/solution.py
+++ b/solution.py
@@ -12,7 +12,8 @@
 MESH = pl.DeviceIdType.MESH
 CHUNK = 128
 AHEAD = 6
-TRAIL = 3
+EARLY = 3
+TRAIL = 6
 ROWS = 256
 
 
@@ -131,10 +132,6 @@
         for copy in loads(i):
             copy.start()
 
-    @pl.when(outer)
-    def _():
-        token_copy().start()
-
     own_tokens = pltpu.make_async_copy(token_hbm, token.at[0], token_load)
 
     @pl.when(inner)
@@ -169,9 +166,14 @@
             def _():
                 weight_copy(z, i, weight_send, 0, mate).start()
 
-        j = i - lag
-
-        @pl.when(jnp.logical_and(inner, jnp.logical_and(j >= 0, j < count)))
+                @pl.when(i == EARLY - 1)
+                def _():
+                    token_copy().start()
+
+        early = i < EARLY + 3
+        j = jnp.where(early, i - 3, i - lag)
+
+        @pl.when(jnp.logical_and(inner, jnp.logical_and(j >= jnp.where(early, 0, EARLY), j < count)))
         def _():
             weight_copy(mate_at, j, pass_send, 0, across).wait_recv()
             weight_copy(mate_at, j, pass_send, 2, across).start()
@@ -187,7 +189,7 @@
 
             weight_copy(across_at, k, weight_send, 1, across).wait_recv()
             weight_copy(3 - mate_at, k, pass_send, 2, across).wait_recv()
-            for owner, result in enumerate((probe, mate_probe)):
+            def project(owner, result):
                 @pl.loop(0, rows // ROWS)
                 def _(b):
                     span = pl.ds(pl.multiple_of(b * ROWS, ROWS), ROWS)
@@ -200,7 +202,9 @@
                         )
                     result[k, span, :] = total.astype(jnp.bfloat16)
 
+            project(1, mate_probe)
             probe_copy(k).start()
+            project(0, probe)
 
     pltpu.make_async_copy(theirs, theirs, pair_send).wait()
     pltpu.make_async_copy(weight.at[0], weight.at[0], weight_send).wait()

time: 184 us -> 183 us (level)
  no operation moved by 1% of the time
where the time goes in v3:
time: 183 us
  Pallas kernels  182 us (99%)
    pallas_call x1, Pallas kernels, line_body(): pl.pallas_call(functools.partial(line_kernel, CHUNK, lag), out_shape=(plt...  176 us
    pallas_call x1, Pallas kernels, line_body(): pl.pallas_call(functools.partial(store_kernel, CHUNK), out_shape=(jax.Sha...  6.25 us

profile of v3, /device:TPU:0, one launch (start us, length us, event | category | flops | bytes accessed | tf_op | source)
XLA Modules:
  0.0 183.1 jit_solution(3137098289634691420)
XLA Ops:
  0.6 176.2 %shard_map.67 = (f32[28,512,128]{2,1,0:T(8,128)S(1)}, f32[28,512,128]{2,1,0:T(8,128)S(1)}, bf16[28,512,128]{2,1,0:T(8,128)(2,1)S(1)}) custom-call(bf16[512,7168]{1,0:T(8,128)(2,1)} %bitcast.7, f32[512,3584]{1,0:T(8,128)} %bitcast.8, f32[512,3584]{1,0:T(8,128)} %bitcast.9, bf16[512,2048]{1,0:T(8,128)(2,1)} %bitcast.10), custom_call_target="tpu_custom_call" | custom-call | tf_op jit(solution)/shard_map/pallas_call | solution.py:245
  176.8 6.2 %shard_map.68 = (f32[512,3584]{1,0:T(8,128)}, f32[512,3584]{1,0:T(8,128)}, bf16[512,3584]{1,0:T(8,128)(2,1)}) custom-call(f32[28,512,128]{2,1,0:T(8,128)S(1)} %get-tuple-element.9.refs_0_, f32[28,512,128]{2,1,0:T(8,128)S(1)} %get-tuple-element.10.refs_1_, bf16[28,512,128]{2,1,0:T(8,128)(2,1)S(1)} %get-tuple-element.11.refs_2_), custom_call_target="tpu_custom_call" | custom-call | tf_op jit(solution)/shard_map/pallas_call | solution.py:272
